TPU v7x, 32 devices: a whole 2x2x4 slice. The times are simulated.
32 devices in a mesh: groups: 2 (over y), expert: 4 (over z), seq: 4 (over x, core).
Axes of the slice: x: 2, y: 2, z: 4, core: 2. Of those that a mesh axis runs over, the one named last changes fastest.
Arguments:
- inputs: bfloat16 [4096, 1024], P(('groups', 'expert', 'seq')), parts along dimension 0, may hold values from -6 to 6
- grad_out: bfloat16 [4096, 1024], P(('groups', 'expert', 'seq')), parts along dimension 0, may hold values from -4 to 4
- gates: bfloat16 [4096, 4], P(('groups', 'expert', 'seq')), parts along dimension 0, may hold values from 0.049804688 to 0.59765625
- expert_ids: int32 [4096, 4], P(('groups', 'expert', 'seq')), parts along dimension 0, may hold values from 0 to 3, as said below
- slot_index: int32 [4096, 4], P(('groups', 'expert', 'seq')), parts along dimension 0, may hold values from 0 to 127, as said below
- filter_taps: bfloat16 [256, 1024], replicated, may hold values from -0.375 to 0.375
- w_gate: bfloat16 [4, 1024, 512], P('expert', 'seq'), may hold values from -0.1875 to 0.1875
- w_up: bfloat16 [4, 1024, 512], P('expert', 'seq'), may hold values from -0.1875 to 0.1875
- w_down: bfloat16 [4, 512, 1024], P('expert', 'seq'), may hold values from -0.25 to 0.25
Outputs:
- grad_inputs: bfloat16 [4096, 1024], P(('groups', 'expert', 'seq')), parts along dimension 0
- grad_gates: bfloat16 [4096, 4], P(('groups', 'expert', 'seq')), parts along dimension 0
- grad_filter: float32 [512, 1024], P('groups'), parts along dimension 0
- grad_w_gate: bfloat16 [8, 1024, 512], P(('groups', 'expert'), 'seq'), parts along dimension 0
- grad_w_up: bfloat16 [8, 1024, 512], P(('groups', 'expert'), 'seq'), parts along dimension 0
- grad_w_down: bfloat16 [8, 512, 1024], P(('groups', 'expert'), 'seq'), parts along dimension 0
There are 2 independent parts, one for each index of `groups`. A program takes and returns all parts, laid end to end along the dimension named above; an argument that names none is the same for every part. Nothing has to cross between parts.
Inputs may be any that keep to these rules, and one draw needn't show every extreme that they name: `expert_ids`: each row names 4 different experts, and every expert is named by some row. Among the assignments of the 128 rows of one device that name the same expert, slot_index takes each of the values 0, 1, ... once, in an order of priority that is not row order; assignments with a slot of 128 or more are dropped.
All inputs are finite; a program needn't handle non-finite values.
Results may differ from a plain program's by a relative error of at most 0.009.
Values may be sent and summed in bfloat16 or wider, within the bound.
A program may use at most 64 MiB of HBM per device.

v0:
```python
import jax
import jax.numpy as jnp
from jax import lax
from jax.sharding import PartitionSpec as P


def from_behind(block, axis, distance):
    devices = range(lax.axis_size(axis))
    route = [(i - distance, i) for i in devices if i - distance in devices]
    return lax.ppermute(block, axis, route)


def depthwise(signal, kernel):
    return lax.conv_general_dilated(
        signal[None],
        kernel[:, None, :],
        (1,),
        "VALID",
        dimension_numbers=("NWC", "WIO", "NWC"),
        feature_group_count=signal.shape[1],
        preferred_element_type=jnp.float32,
    )[0]


def contract(left, right, left_dim, right_dim):
    return lax.dot_general(
        left, right, (((left_dim,), (right_dim,)), ((), ())), preferred_element_type=jnp.float32
    )


def expert_pass(token_rows, scaled_rows, gate_mat, up_mat, down_mat):
    pre_gate = jnp.dot(token_rows, gate_mat, preferred_element_type=jnp.float32)
    pre_up = jnp.dot(token_rows, up_mat, preferred_element_type=jnp.float32)
    sigma = jax.nn.sigmoid(pre_gate)
    swish = pre_gate * sigma
    hidden = (swish * pre_up).astype(jnp.bfloat16)
    outputs = jnp.dot(hidden, down_mat, preferred_element_type=jnp.float32).astype(jnp.bfloat16)
    grad_hidden = contract(scaled_rows, down_mat, 1, 1)
    grad_pre_gate = (grad_hidden * pre_up * (sigma * (1.0 + pre_gate * (1.0 - sigma)))).astype(
        jnp.bfloat16
    )
    grad_pre_up = (grad_hidden * swish).astype(jnp.bfloat16)
    part_gate = contract(token_rows, grad_pre_gate, 0, 0)
    part_up = contract(token_rows, grad_pre_up, 0, 0)
    part_down = contract(hidden, scaled_rows, 0, 0)
    grad_rows = (
        contract(grad_pre_gate, gate_mat, 1, 1) + contract(grad_pre_up, up_mat, 1, 1)
    ).astype(jnp.bfloat16)
    return (grad_rows, outputs, (part_gate, part_up, part_down))


def body(inputs, grad_out, gates, expert_ids, slot_index, filter_taps, w_gate, w_up, w_down):
    tok_count, width = inputs.shape
    taps = filter_taps.shape[0]
    top_count = expert_ids.shape[1]
    experts = lax.axis_size("expert")
    capacity = tok_count * top_count // experts
    reach = taps - 1
    shift_count = (reach + tok_count - 1) // tok_count
    earlier = [from_behind(inputs, "seq", shift_by) for shift_by in range(shift_count, 0, -1)]
    extended = jnp.concatenate(earlier + [inputs], axis=0)[-(tok_count + reach) :]
    filtered = depthwise(extended, filter_taps[::-1]).astype(jnp.bfloat16)
    kept = slot_index < capacity
    dest = jnp.where(kept, expert_ids * capacity + slot_index, experts * capacity).reshape(-1)

    def place(values):
        rest = values.shape[1:]
        empty = jnp.zeros((experts * capacity,) + rest, values.dtype)
        return empty.at[dest].set(values, mode="drop").reshape((experts, capacity) + rest)

    def fetch(buffer):
        rest = buffer.shape[2:]
        flat = buffer.reshape((experts * capacity,) + rest)
        return jnp.take(flat, dest, axis=0, mode="fill", fill_value=0).reshape(
            (tok_count, top_count) + rest
        )

    token_send = place(
        jnp.broadcast_to(filtered[:, None, :], (tok_count, top_count, width)).reshape(-1, width)
    )
    gate_full, up_full, down_full = (
        lax.all_gather(w_gate, "seq", axis=1, tiled=True),
        lax.all_gather(w_up, "seq", axis=1, tiled=True),
        lax.all_gather(w_down, "seq", axis=1, tiled=True),
    )
    gate_mat = gate_full[0]
    up_mat = up_full[0]
    down_mat = down_full[0]
    scaled = (
        gates.astype(jnp.float32)[:, :, None] * grad_out.astype(jnp.float32)[:, None, :]
    ).astype(jnp.bfloat16)
    token_recv, scaled_recv = (
        lax.all_to_all(token_send, "expert", split_axis=0, concat_axis=0, tiled=True),
        lax.all_to_all(
            place(scaled.reshape(-1, width)), "expert", split_axis=0, concat_axis=0, tiled=True
        ),
    )
    grad_rows, outputs, partials = expert_pass(
        token_recv.reshape(-1, width), scaled_recv.reshape(-1, width), gate_mat, up_mat, down_mat
    )
    grad_back, output_back = (
        lax.all_to_all(
            grad_rows.reshape(experts, capacity, width),
            "expert",
            split_axis=0,
            concat_axis=0,
            tiled=True,
        ),
        lax.all_to_all(
            outputs.reshape(experts, capacity, width),
            "expert",
            split_axis=0,
            concat_axis=0,
            tiled=True,
        ),
    )
    output_rows = fetch(output_back)
    grad_gates = jnp.sum(
        grad_out.astype(jnp.float32)[:, None, :] * output_rows.astype(jnp.float32), axis=2
    ).astype(jnp.bfloat16)
    summed_gate, summed_up, summed_down = (
        lax.psum_scatter(
            partials[0][None].astype(jnp.bfloat16), "seq", scatter_dimension=1, tiled=True
        ).astype(jnp.float32),
        lax.psum_scatter(
            partials[1][None].astype(jnp.bfloat16), "seq", scatter_dimension=1, tiled=True
        ).astype(jnp.float32),
        lax.psum_scatter(
            partials[2][None].astype(jnp.bfloat16), "seq", scatter_dimension=1, tiled=True
        ).astype(jnp.float32),
    )
    grad_filtered = jnp.sum(fetch(grad_back).astype(jnp.float32), axis=1).astype(jnp.bfloat16)
    later = [from_behind(grad_filtered, "seq", -shift_by) for shift_by in range(1, shift_count + 1)]
    grad_extended = jnp.concatenate([grad_filtered] + later, axis=0)[: tok_count + reach]
    grad_inputs = depthwise(grad_extended, filter_taps).astype(jnp.bfloat16)
    local_taps = depthwise(extended, grad_filtered)[::-1]
    grad_filter = lax.psum(local_taps, ("expert", "seq"))
    return (
        grad_inputs,
        grad_gates,
        grad_filter,
        summed_gate.astype(jnp.bfloat16),
        summed_up.astype(jnp.bfloat16),
        summed_down.astype(jnp.bfloat16),
    )


def solution(mesh):
    return jax.shard_map(
        body,
        mesh=mesh,
        in_specs=(
            P(("groups", "expert", "seq"), None),
            P(("groups", "expert", "seq"), None),
            P(("groups", "expert", "seq"), None),
            P(("groups", "expert", "seq"), None),
            P(("groups", "expert", "seq"), None),
            P(),
            P("expert", "seq", None),
            P("expert", "seq", None),
            P("expert", "seq", None),
        ),
        out_specs=(
            P(("groups", "expert", "seq"), None),
            P(("groups", "expert", "seq"), None),
            P("groups", None),
            P(("groups", "expert"), "seq", None),
            P(("groups", "expert"), "seq", None),
            P(("groups", "expert"), "seq", None),
        ),
        check_vma=False,
    )
```

profile of v0, /device:TPU:0, one launch (start us, length us, event | category | flops | bytes accessed | tf_op | source)
XLA Modules:
  0.0 352.4 jit_solution(16538734937356647307)
XLA Ops:
  7.9 5.6 %collective-permute-start = (bf16[128,1024]{1,0:T(8,128)(2,1)}, bf16[128,1024]{1,0:T(8,128)(2,1)}, u32[]{:S(2)}, u32[]{:S(2)}) collective-permute-start(bf16[128,1024]{1,0:T(8,128)(2,1)} %param.11), channel_id=1, source_target_pairs={{0,2},{1,3},{4,6},{5,7},{8,10},{9,11},{12,14},{13,15},{16,18},{17,... | collective-permute-start | bytes 786440 | tf_op jit(solution)/shard_map/ppermute | solution.py:10
  13.5 2.2 collective-permute-start.1
  17.5 2.8 mul.55
  22.3 3.6 %scatter_custom_fusion = bf16[512,1024]{1,0:T(8,128)(2,1)} fusion(s32[512]{0:T(512)S(1)} %bitcast.76, f32[512,1024]{1,0:T(8,128)S(1)} %mul.56, f32[512]{0:T(512)S(1)} %reshape.113, bf16[]{:T(256)} %constant.7.clone.1), kind=kCustom, calls=%fused_computation.21 | custom fusion | flops 1048576 | bytes 3147778 | tf_op jit(solution)/shard_map/scatter | solution.py:69
  25.9 5.0 %all-to-all-start = ((bf16[4,128,1024]{2,1,0:T(8,128)(2,1)}), bf16[4,128,1024]{2,1,0:T(8,128)(2,1)}, u32[]{:S(2)}, u32[]{:S(2)}) async-start(bf16[4,128,1024]{2,1,0:T(8,128)(2,1)} %bitcast.1), calls=%async_computation | async-start | bytes 2097152 | tf_op jit(solution)/shard_map/all_to_all | solution.py:94
  33.6 14.0 %convolution_convert_fusion.4 = bf16[1,128,1024]{2,0,1:T(2,128)(2,1)S(1)} fusion(bf16[1,383,1024]{2,1,0:T(8,128)(2,1)S(1)} %fusion.27, bf16[256,1,1024]{2,0,1:T(8,128)(2,1)S(1)} %bitcast.74), kind=kOutput, calls=%fused_computation.17 | convolution fusion | flops 67239936 | bytes 1570816 | tf_op jit(solution)/shard_map/conv_general_dilated | solution.py:14
  49.1 4.2 %scatter_custom_fusion.1 = bf16[512,1024]{1,0:T(8,128)(2,1)} fusion(s32[512]{0:T(512)S(1)} %bitcast.77, bf16[512,1024]{1,0:T(8,128)(2,1)} %reshape.142, bf16[]{:T(256)} %constant.7.clone.1), kind=kCustom, calls=%fused_computation.49 | custom fusion | bytes 1049088 | tf_op jit(solution)/shard_map/scatter | solution.py:69
  53.4 2.9 all-to-all-done
  56.3 3.5 all-to-all-start.1
  60.6 3.3 fusion.20
  63.8 21.2 %all-to-all-done.1 = bf16[4,128,1024]{2,1,0:T(8,128)(2,1)S(1)} async-done(((bf16[4,128,1024]{2,1,0:T(8,128)(2,1)}), bf16[4,128,1024]{2,1,0:T(8,128)(2,1)S(1)}, u32[]{:S(2)}, u32[]{:S(2)}) %all-to-all-start.1) | async-done | bytes 1048608 | tf_op jit(solution)/shard_map/all_to_all | solution.py:93
  86.0 2.9 fusion.14
  88.9 4.1 %multiply_convert_fusion.2 = (bf16[512,512]{1,0:T(8,128)(2,1)}, bf16[512,512]{1,0:T(8,128)(2,1)S(1)}, bf16[512,512]{1,0:T(8,128)(2,1)S(1)}) fusion(f32[512,512]{1,0:T(8,128)} %fusion.14, f32[512,512]{1,0:T(8,128)} %fusion.20, bf16[512,1024]{1,0:T(8,128)(2,1)} %bitcast.68, bf16[1,1024,512]{2,1,0:T(8,128)(2,1)} %all-gather.6.cloned.1.call-done), kind=kOutput, calls=%fused_computation.35 | convolution fusion | flops 540803072 | bytes 5767168 | tf_op jit(solution)/shard_map/dot_general | solution.py:33
  96.3 3.5 all-to-all-start.2
  100.0 25.0 %all-to-all-done.2 = bf16[4,128,1024]{2,1,0:T(8,128)(2,1)S(1)} async-done(((bf16[4,128,1024]{2,1,0:T(8,128)(2,1)}), bf16[4,128,1024]{2,1,0:T(8,128)(2,1)S(1)}, u32[]{:S(2)}, u32[]{:S(2)}) %all-to-all-start.2) | async-done | bytes 1048608 | tf_op jit(solution)/shard_map/all_to_all | solution.py:102
  125.0 2.8 gather_fusion
  130.4 2.5 reduce_sum.21
  132.9 15.1 %fusion.8 = f32[1,256,1024]{2,0,1:T(1,128)S(1)} fusion(bf16[1,383,1024]{2,1,0:T(8,128)(2,1)} %copy-done.4, bf16[128,1,1024]{2,0,1:T(8,128)(2,1)S(1)} %bitcast.72), kind=kOutput, calls=%fused_computation.18 | convolution fusion | flops 67108864 | bytes 2095104 | tf_op jit(solution)/shard_map/conv_general_dilated | solution.py:14
  148.2 5.3 %rev.7 = f32[256,1024]{1,0:T(8,128)} reverse(f32[256,1024]{1,0:T(8,128)S(1)} %bitcast.64), dimensions={0} | reverse | bytes 2097152 | tf_op jit(solution)/shard_map/rev | solution.py:136
  153.6 3.2 fusion.4
  156.9 2.8 fusion.3
  159.7 3.1 convolution_convert_fusion.3
  162.8 3.5 all-to-all-start.3
  169.2 3.1 fusion.2
  172.3 22.6 %all-to-all-done.3 = bf16[4,128,1024]{2,1,0:T(8,128)(2,1)S(1)} async-done(((bf16[4,128,1024]{2,1,0:T(8,128)(2,1)}), bf16[4,128,1024]{2,1,0:T(8,128)(2,1)S(1)}, u32[]{:S(2)}, u32[]{:S(2)}) %all-to-all-start.3) | async-done | bytes 1048608 | tf_op jit(solution)/shard_map/all_to_all | solution.py:109
  194.8 2.8 gather_fusion.1
  201.2 14.0 %fusion.5 = bf16[1,128,1024]{2,0,1:T(2,128)(2,1)S(1)} fusion(bf16[1,383,1024]{2,1,0:T(8,128)(2,1)S(1)} %fusion.26, bf16[256,1,1024]{2,0,1:T(8,128)(2,1)S(1)} %bitcast.73), kind=kOutput, calls=%fused_computation.16 | convolution fusion | flops 67239936 | bytes 1570816 | tf_op jit(solution)/shard_map/conv_general_dilated | solution.py:14
  216.0 44.2 %all-reduce.2.cloned.1.call-done = f32[256,1024]{1,0:T(8,128)} async-done(((f32[256,1024]{1,0:T(8,128)}), f32[256,1024]{1,0:T(8,128)}) %all-reduce.2.cloned.1.call-update) | async-done | bytes 1048592 | tf_op jit(solution)/shard_map/psum | solution.py:137
  260.1 27.1 %reduce-scatter.8.cloned.1.call-done = bf16[1,128,1024]{2,1,0:T(8,128)(2,1)} async-done(((bf16[1,512,1024]{2,1,0:T(8,128)(2,1)}), bf16[1,128,1024]{2,1,0:T(8,128)(2,1)}) %reduce-scatter.8.cloned.1.call-update) | async-done | bytes 262160 | tf_op jit(solution)/shard_map/reduce_scatter | solution.py:128
  287.2 28.0 %reduce-scatter.6.cloned.1.call-done = bf16[1,256,512]{2,1,0:T(8,128)(2,1)} async-done(((bf16[1,1024,512]{2,1,0:T(8,128)(2,1)}), bf16[1,256,512]{2,1,0:T(8,128)(2,1)}) %reduce-scatter.6.cloned.1.call-update) | async-done | bytes 262160 | tf_op jit(solution)/shard_map/reduce_scatter | solution.py:125
  315.3 28.0 %reduce-scatter.4.cloned.1.call-done = bf16[1,256,512]{2,1,0:T(8,128)(2,1)} async-done(((bf16[1,1024,512]{2,1,0:T(8,128)(2,1)}), bf16[1,256,512]{2,1,0:T(8,128)(2,1)}) %reduce-scatter.4.cloned.1.call-update) | async-done | bytes 262160 | tf_op jit(solution)/shard_map/reduce_scatter | solution.py:122
  343.3 2.3 copy.52
  (69 shorter events, 24.0 us)
Async XLA Ops:
  7.2 53.4 %all-gather.4.cloned.1.call-start = ((), (), s32[]{:S(2)}) async-start(), calls=%async_computation.7 | async-start | bytes 1310720 | tf_op jit(solution)/shard_map/all_gather | solution.py:84
  7.9 24.5 %collective-permute-start = (bf16[128,1024]{1,0:T(8,128)(2,1)}, bf16[128,1024]{1,0:T(8,128)(2,1)}, u32[]{:S(2)}, u32[]{:S(2)}) collective-permute-start(bf16[128,1024]{1,0:T(8,128)(2,1)} %param.11), channel_id=1, source_target_pairs={{0,2},{1,3},{4,6},{5,7},{8,10},{9,11},{12,14},{13,15},{16,18},{17,... | collective-permute-start | bytes 786440 | tf_op jit(solution)/shard_map/ppermute | solution.py:10
  13.5 18.9 %collective-permute-start.1 = (bf16[128,1024]{1,0:T(8,128)(2,1)}, bf16[128,1024]{1,0:T(8,128)(2,1)}, u32[]{:S(2)}, u32[]{:S(2)}) collective-permute-start(bf16[128,1024]{1,0:T(8,128)(2,1)} %param.11), channel_id=1, source_target_pairs={{0,1},{1,2},{2,3},{4,5},{5,6},{6,7},{8,9},{9,10},{10,11},{12,13},{... | collective-permute-start | bytes 786440 | tf_op jit(solution)/shard_map/ppermute | solution.py:10
  22.3 9.4 %copy-start.7 = (bf16[256,1024]{1,0:T(8,128)(2,1)S(1)}, bf16[256,1024]{1,0:T(8,128)(2,1)}, u32[]{:S(2)}) copy-start(bf16[256,1024]{1,0:T(8,128)(2,1)} %param.16) | copy-start | bytes 1572868
  25.9 6.5 %copy-start.9 = (bf16[128,1024]{1,0:T(8,128)(2,1)S(1)}, bf16[128,1024]{1,0:T(8,128)(2,1)}, u32[]{:S(2)}) copy-start(bf16[128,1024]{1,0:T(8,128)(2,1)} %param.11) | copy-start | bytes 786436
  25.9 30.3 %all-to-all-start = ((bf16[4,128,1024]{2,1,0:T(8,128)(2,1)}), bf16[4,128,1024]{2,1,0:T(8,128)(2,1)}, u32[]{:S(2)}, u32[]{:S(2)}) async-start(bf16[4,128,1024]{2,1,0:T(8,128)(2,1)} %bitcast.1), calls=%async_computation | async-start | bytes 2097152 | tf_op jit(solution)/shard_map/all_to_all | solution.py:94
  30.9 32.9 %all-gather.8.cloned.1.call-start = ((), (), s32[]{:S(2)}) async-start(), calls=%async_computation.9 | async-start | bytes 1310720 | tf_op jit(solution)/shard_map/all_gather | solution.py:82
  33.6 14.0 %copy-start.4 = (bf16[1,383,1024]{2,1,0:T(8,128)(2,1)}, bf16[1,383,1024]{2,1,0:T(8,128)(2,1)S(1)}, u32[]{:S(2)}) copy-start(bf16[1,383,1024]{2,1,0:T(8,128)(2,1)S(1)} %fusion.27) | copy-start | bytes 2353156
  56.3 28.7 %all-to-all-start.1 = ((bf16[4,128,1024]{2,1,0:T(8,128)(2,1)}), bf16[4,128,1024]{2,1,0:T(8,128)(2,1)S(1)}, u32[]{:S(2)}, u32[]{:S(2)}) async-start(bf16[4,128,1024]{2,1,0:T(8,128)(2,1)} %bitcast.6), calls=%async_computation.1 | async-start | bytes 2097152 | tf_op jit(solution)/shard_map/all_to_all | solution.py:93
  59.8 29.1 %all-gather.6.cloned.1.call-start = ((), (), s32[]{:S(2)}) async-start(), calls=%async_computation.8 | async-start | bytes 1310720 | tf_op jit(solution)/shard_map/all_gather | solution.py:83
  85.0 1.0 copy-start.1
  88.9 4.1 %copy-start = (bf16[1,1024,512]{2,1,0:T(8,128)(2,1)S(1)}, bf16[1,1024,512]{2,1,0:T(8,128)(2,1)}, u32[]{:S(2)}) copy-start(bf16[1,1024,512]{2,1,0:T(8,128)(2,1)} %all-gather.8.cloned.1.call-done) | copy-start | bytes 3145732
  93.0 0.8 copy-start.5
  93.0 3.3 copy-start.6
  93.0 1.6 copy-start.3
  96.3 28.7 %all-to-all-start.2 = ((bf16[4,128,1024]{2,1,0:T(8,128)(2,1)}), bf16[4,128,1024]{2,1,0:T(8,128)(2,1)S(1)}, u32[]{:S(2)}, u32[]{:S(2)}) async-start(bf16[4,128,1024]{2,1,0:T(8,128)(2,1)} %bitcast.65), calls=%async_computation.2 | async-start | bytes 2097152 | tf_op jit(solution)/shard_map/all_to_all | solution.py:102
  99.8 160.3 %all-reduce.2.cloned.1.call-start = ((), (), s32[]{:S(2)}) async-start(), calls=%async_computation.10 | async-start | bytes 2097152 | tf_op jit(solution)/shard_map/psum | solution.py:137
  153.5 3.3 copy-start.2
  153.5 133.7 %reduce-scatter.8.cloned.1.call-start = ((), (), s32[]{:S(2)}) async-start(), calls=%async_computation.13 | async-start | bytes 1310720 | tf_op jit(solution)/shard_map/reduce_scatter | solution.py:128
  156.8 158.5 %reduce-scatter.6.cloned.1.call-start = ((), (), s32[]{:S(2)}) async-start(), calls=%async_computation.12 | async-start | bytes 1310720 | tf_op jit(solution)/shard_map/reduce_scatter | solution.py:125
  162.8 32.1 %all-to-all-start.3 = ((bf16[4,128,1024]{2,1,0:T(8,128)(2,1)}), bf16[4,128,1024]{2,1,0:T(8,128)(2,1)S(1)}, u32[]{:S(2)}, u32[]{:S(2)}) async-start(bf16[4,128,1024]{2,1,0:T(8,128)(2,1)} %bitcast.71), calls=%async_computation.3 | async-start | bytes 2097152 | tf_op jit(solution)/shard_map/all_to_all | solution.py:109
  166.3 177.0 %reduce-scatter.4.cloned.1.call-start = ((), (), s32[]{:S(2)}) async-start(), calls=%async_computation.11 | async-start | bytes 1310720 | tf_op jit(solution)/shard_map/reduce_scatter | solution.py:122
  166.3 33.8 %collective-permute-start.3 = (bf16[128,1024]{1,0:T(8,128)(2,1)S(1)}, bf16[128,1024]{1,0:T(8,128)(2,1)}, u32[]{:S(2)}, u32[]{:S(2)}) collective-permute-start(bf16[128,1024]{1,0:T(8,128)(2,1)S(1)} %reduce_sum.21), channel_id=1, source_target_pairs={{2,0},{3,1},{6,4},{7,5},{10,8},{11,9},{14,12},{15,13},{18,16},{19,... | collective-permute-start | bytes 786440 | tf_op jit(solution)/shard_map/ppermute | solution.py:10
  167.6 32.5 %collective-permute-start.2 = (bf16[128,1024]{1,0:T(8,128)(2,1)S(1)}, bf16[128,1024]{1,0:T(8,128)(2,1)}, u32[]{:S(2)}, u32[]{:S(2)}) collective-permute-start(bf16[128,1024]{1,0:T(8,128)(2,1)S(1)} %reduce_sum.21), channel_id=1, source_target_pairs={{1,0},{2,1},{3,2},{5,4},{6,5},{7,6},{9,8},{10,9},{11,10},{13,12},{... | collective-permute-start | bytes 786440 | tf_op jit(solution)/shard_map/ppermute | solution.py:10
  197.6 3.6 %copy-start.8 = (bf16[256,1024]{1,0:T(8,128)(2,1)S(1)}, bf16[256,1024]{1,0:T(8,128)(2,1)}, u32[]{:S(2)}) copy-start(bf16[256,1024]{1,0:T(8,128)(2,1)} %param.16) | copy-start | bytes 1572868
Sparse Core Ops, SparseCore 0:
  9.6 19.4 all-gather.3
  33.3 17.2 all-gather.7
  62.2 17.1 all-gather.5
  153.6 106.4 all-reduce.1
  263.1 24.1 reduce-scatter.7
  290.3 24.8 reduce-scatter.5
  318.4 24.8 reduce-scatter.3
where the time goes:
time: 353 us; the launch traced here: 352 us
  waiting for transfers between devices  201 us (57%)
  matrix products  67.9 us (19%)
  local copies, waits for them, and re-layouts  30.4 us (9%)
  starting transfers between devices  26.5 us (8%)
  between operations  14.4 us (4%)
  other arithmetic  12.2 us (3%)
    psum x1, waiting for transfers between devices, body(): grad_filter = lax.psum(local_taps, ('expert', 'seq'))  44.2 us
    conv_general_dilated x3, matrix products, depthwise(): lax.conv_general_dilated(signal[None], kernel[:, None, :], (1,), 'VALID',...  43 us
    reduce_scatter x1, waiting for transfers between devices, body(): lax.psum_scatter(partials[1][None].astype(jnp.bfloat16), 'seq', scatter_d...  28 us
    reduce_scatter x1, waiting for transfers between devices, body(): lax.psum_scatter(partials[0][None].astype(jnp.bfloat16), 'seq', scatter_d...  28 us
    reduce_scatter x1, waiting for transfers between devices, body(): lax.psum_scatter(partials[2][None].astype(jnp.bfloat16), 'seq', scatter_d...  27.1 us
    all_to_all x1, waiting for transfers between devices, body(): lax.all_to_all(grad_rows.reshape(experts, capacity, width), 'expert', spl...  25 us
    all_to_all x1, waiting for transfers between devices, body(): lax.all_to_all(outputs.reshape(experts, capacity, width), 'expert', split...  22.6 us
    all_to_all x1, waiting for transfers between devices, body(): lax.all_to_all(token_send, 'expert', split_axis=0, concat_axis=0, tiled=T...  21.2 us
  transfers between devices with their start and end apart: 15, of which 8 were waited for; matrix products, arithmetic and copies ran while one was open for 20% of the time, Pallas kernels for 0%

commit v1 on v0

--- a/solution.py
+++ b/solution.py
@@ -134,7 +134,9 @@
     grad_extended = jnp.concatenate([grad_filtered] + later, axis=0)[: tok_count + reach]
     grad_inputs = depthwise(grad_extended, filter_taps).astype(jnp.bfloat16)
     local_taps = depthwise(extended, grad_filtered)[::-1]
-    grad_filter = lax.psum(local_taps, ("expert", "seq"))
+    grad_filter = local_taps
+    for mesh_axis in ("seq", "expert"):
+        grad_filter = lax.psum(grad_filter, mesh_axis)
     return (
         grad_inputs,
         grad_gates,

time: 353 us -> 339 us (0.960)
  waiting for transfers between devices: 201 us -> 187 us
    reduce_scatter x1, waiting for transfers between devices: 27.1 us -> 3.15 us  [body(): lax.psum_scatter(partials[2][None].astype(jnp.bfloat16), 'seq', scatter_d...]
    psum x1 -> x2, waiting for transfers between devices: 44.2 us -> 54.3 us  [body(): grad_filter = lax.psum(grad_filter, mesh_axis)]
  transfers between devices with their start and end apart: 15 -> 16, of which waited for: 8 -> 8; matrix products, arithmetic and copies ran while one was open for 20% -> 21% of each run, Pallas kernels for 0% -> 0%
where the time goes in v1:
time: 339 us; the launch traced here: 338 us
  waiting for transfers between devices  187 us (55%)
  matrix products  67.6 us (20%)
  local copies, waits for them, and re-layouts  30.4 us (9%)
  starting transfers between devices  26.5 us (8%)
  between operations  14.4 us (4%)
  other arithmetic  12.2 us (4%)
    psum x2, waiting for transfers between devices, body(): grad_filter = lax.psum(grad_filter, mesh_axis)  54.3 us
    conv_general_dilated x3, matrix products, depthwise(): lax.conv_general_dilated(signal[None], kernel[:, None, :], (1,), 'VALID',...  43 us
    reduce_scatter x1, waiting for transfers between devices, body(): lax.psum_scatter(partials[0][None].astype(jnp.bfloat16), 'seq', scatter_d...  28.2 us
    reduce_scatter x1, waiting for transfers between devices, body(): lax.psum_scatter(partials[1][None].astype(jnp.bfloat16), 'seq', scatter_d...  27.9 us
    all_to_all x1, waiting for transfers between devices, body(): lax.all_to_all(grad_rows.reshape(experts, capacity, width), 'expert', spl...  25 us
    all_to_all x1, waiting for transfers between devices, body(): lax.all_to_all(outputs.reshape(experts, capacity, width), 'expert', split...  22.3 us
    all_to_all x1, waiting for transfers between devices, body(): lax.all_to_all(token_send, 'expert', split_axis=0, concat_axis=0, tiled=T...  21.1 us
    dot_general x6, matrix products, contract(): lax.dot_general(left, right, (((left_dim,), (right_dim,)), ((), ())), pre...  14.5 us
  transfers between devices with their start and end apart: 16, of which 8 were waited for; matrix products, arithmetic and copies ran while one was open for 21% of the time, Pallas kernels for 0%

profile of v1, /device:TPU:0, one launch (start us, length us, event | category | flops | bytes accessed | tf_op | source)
XLA Modules:
  0.0 338.0 jit_solution(5260260139604690959)
XLA Ops:
  7.9 5.6 %collective-permute-start = (bf16[128,1024]{1,0:T(8,128)(2,1)}, bf16[128,1024]{1,0:T(8,128)(2,1)}, u32[]{:S(2)}, u32[]{:S(2)}) collective-permute-start(bf16[128,1024]{1,0:T(8,128)(2,1)} %param.11), channel_id=1, source_target_pairs={{0,2},{1,3},{4,6},{5,7},{8,10},{9,11},{12,14},{13,15},{16,18},{17,... | collective-permute-start | bytes 786440 | tf_op jit(solution)/shard_map/ppermute | solution.py:10
  13.5 2.1 collective-permute-start.1
  17.4 2.8 mul.55
  22.3 3.7 %scatter_custom_fusion = bf16[512,1024]{1,0:T(8,128)(2,1)} fusion(s32[512]{0:T(512)S(1)} %bitcast.76, f32[512,1024]{1,0:T(8,128)S(1)} %mul.56, f32[512]{0:T(512)S(1)} %reshape.113, bf16[]{:T(256)} %constant.7.clone.1), kind=kCustom, calls=%fused_computation.21 | custom fusion | flops 1048576 | bytes 3147778 | tf_op jit(solution)/shard_map/scatter | solution.py:69
  25.9 5.0 %all-to-all-start = ((bf16[4,128,1024]{2,1,0:T(8,128)(2,1)}), bf16[4,128,1024]{2,1,0:T(8,128)(2,1)}, u32[]{:S(2)}, u32[]{:S(2)}) async-start(bf16[4,128,1024]{2,1,0:T(8,128)(2,1)} %bitcast.1), calls=%async_computation | async-start | bytes 2097152 | tf_op jit(solution)/shard_map/all_to_all | solution.py:94
  33.6 14.0 %convolution_convert_fusion.4 = bf16[1,128,1024]{2,0,1:T(2,128)(2,1)S(1)} fusion(bf16[1,383,1024]{2,1,0:T(8,128)(2,1)S(1)} %fusion.27, bf16[256,1,1024]{2,0,1:T(8,128)(2,1)S(1)} %bitcast.74), kind=kOutput, calls=%fused_computation.17 | convolution fusion | flops 67239936 | bytes 1570816 | tf_op jit(solution)/shard_map/conv_general_dilated | solution.py:14
  49.1 4.2 %scatter_custom_fusion.1 = bf16[512,1024]{1,0:T(8,128)(2,1)} fusion(s32[512]{0:T(512)S(1)} %bitcast.77, bf16[512,1024]{1,0:T(8,128)(2,1)} %reshape.142, bf16[]{:T(256)} %constant.7.clone.1), kind=kCustom, calls=%fused_computation.49 | custom fusion | bytes 1049088 | tf_op jit(solution)/shard_map/scatter | solution.py:69
  53.4 3.0 all-to-all-done
  56.3 3.5 %all-to-all-start.1 = ((bf16[4,128,1024]{2,1,0:T(8,128)(2,1)}), bf16[4,128,1024]{2,1,0:T(8,128)(2,1)S(1)}, u32[]{:S(2)}, u32[]{:S(2)}) async-start(bf16[4,128,1024]{2,1,0:T(8,128)(2,1)} %bitcast.6), calls=%async_computation.1 | async-start | bytes 2097152 | tf_op jit(solution)/shard_map/all_to_all | solution.py:93
  60.6 3.3 fusion.20
  63.9 21.1 %all-to-all-done.1 = bf16[4,128,1024]{2,1,0:T(8,128)(2,1)S(1)} async-done(((bf16[4,128,1024]{2,1,0:T(8,128)(2,1)}), bf16[4,128,1024]{2,1,0:T(8,128)(2,1)S(1)}, u32[]{:S(2)}, u32[]{:S(2)}) %all-to-all-start.1) | async-done | bytes 1048608 | tf_op jit(solution)/shard_map/all_to_all | solution.py:93
  86.0 2.9 fusion.14
  88.9 4.1 %multiply_convert_fusion.2 = (bf16[512,512]{1,0:T(8,128)(2,1)}, bf16[512,512]{1,0:T(8,128)(2,1)S(1)}, bf16[512,512]{1,0:T(8,128)(2,1)S(1)}) fusion(f32[512,512]{1,0:T(8,128)} %fusion.14, f32[512,512]{1,0:T(8,128)} %fusion.20, bf16[512,1024]{1,0:T(8,128)(2,1)} %bitcast.68, bf16[1,1024,512]{2,1,0:T(8,128)(2,1)} %all-gather.6.cloned.1.call-done), kind=kOutput, calls=%fused_computation.35 | convolution fusion | flops 540803072 | bytes 5767168 | tf_op jit(solution)/shard_map/dot_general | solution.py:33
  96.3 3.5 %all-to-all-start.2 = ((bf16[4,128,1024]{2,1,0:T(8,128)(2,1)}), bf16[4,128,1024]{2,1,0:T(8,128)(2,1)S(1)}, u32[]{:S(2)}, u32[]{:S(2)}) async-start(bf16[4,128,1024]{2,1,0:T(8,128)(2,1)} %bitcast.65), calls=%async_computation.2 | async-start | bytes 2097152 | tf_op jit(solution)/shard_map/all_to_all | solution.py:102
  100.0 25.0 %all-to-all-done.2 = bf16[4,128,1024]{2,1,0:T(8,128)(2,1)S(1)} async-done(((bf16[4,128,1024]{2,1,0:T(8,128)(2,1)}), bf16[4,128,1024]{2,1,0:T(8,128)(2,1)S(1)}, u32[]{:S(2)}, u32[]{:S(2)}) %all-to-all-start.2) | async-done | bytes 1048608 | tf_op jit(solution)/shard_map/all_to_all | solution.py:102
  125.0 2.8 gather_fusion
  130.4 2.5 reduce_sum.21
  132.9 15.1 %fusion.8 = f32[1,256,1024]{2,0,1:T(1,128)S(1)} fusion(bf16[1,383,1024]{2,1,0:T(8,128)(2,1)} %copy-done.4, bf16[128,1,1024]{2,0,1:T(8,128)(2,1)S(1)} %bitcast.72), kind=kOutput, calls=%fused_computation.18 | convolution fusion | flops 67108864 | bytes 2095104 | tf_op jit(solution)/shard_map/conv_general_dilated | solution.py:14
  148.2 5.3 %rev.7 = f32[256,1024]{1,0:T(8,128)} reverse(f32[256,1024]{1,0:T(8,128)S(1)} %bitcast.64), dimensions={0} | reverse | bytes 2097152 | tf_op jit(solution)/shard_map/rev | solution.py:136
  153.6 3.2 fusion.4
  156.9 2.8 fusion.3
  159.7 2.8 fusion.2
  162.5 3.1 convolution_convert_fusion.3
  165.6 3.5 %all-to-all-start.3 = ((bf16[4,128,1024]{2,1,0:T(8,128)(2,1)}), bf16[4,128,1024]{2,1,0:T(8,128)(2,1)S(1)}, u32[]{:S(2)}, u32[]{:S(2)}) async-start(bf16[4,128,1024]{2,1,0:T(8,128)(2,1)} %bitcast.71), calls=%async_computation.3 | async-start | bytes 2097152 | tf_op jit(solution)/shard_map/all_to_all | solution.py:109
  172.0 22.3 %all-to-all-done.3 = bf16[4,128,1024]{2,1,0:T(8,128)(2,1)S(1)} async-done(((bf16[4,128,1024]{2,1,0:T(8,128)(2,1)}), bf16[4,128,1024]{2,1,0:T(8,128)(2,1)S(1)}, u32[]{:S(2)}, u32[]{:S(2)}) %all-to-all-start.3) | async-done | bytes 1048608 | tf_op jit(solution)/shard_map/all_to_all | solution.py:109
  194.3 2.8 gather_fusion.1
  200.7 14.0 %fusion.5 = bf16[1,128,1024]{2,0,1:T(2,128)(2,1)S(1)} fusion(bf16[1,383,1024]{2,1,0:T(8,128)(2,1)S(1)} %fusion.26, bf16[256,1,1024]{2,0,1:T(8,128)(2,1)S(1)} %bitcast.73), kind=kOutput, calls=%fused_computation.16 | convolution fusion | flops 67239936 | bytes 1570816 | tf_op jit(solution)/shard_map/conv_general_dilated | solution.py:14
  215.4 3.1 reduce-scatter.8.cloned.1.call-done
  218.6 27.9 %reduce-scatter.6.cloned.1.call-done = bf16[1,256,512]{2,1,0:T(8,128)(2,1)} async-done(((bf16[1,1024,512]{2,1,0:T(8,128)(2,1)}), bf16[1,256,512]{2,1,0:T(8,128)(2,1)}) %reduce-scatter.6.cloned.1.call-update) | async-done | bytes 262160 | tf_op jit(solution)/shard_map/reduce_scatter | solution.py:125
  246.5 28.2 %reduce-scatter.4.cloned.1.call-done = bf16[1,256,512]{2,1,0:T(8,128)(2,1)} async-done(((bf16[1,1024,512]{2,1,0:T(8,128)(2,1)}), bf16[1,256,512]{2,1,0:T(8,128)(2,1)}) %reduce-scatter.4.cloned.1.call-update) | async-done | bytes 262160 | tf_op jit(solution)/shard_map/reduce_scatter | solution.py:122
  274.6 54.2 %all-reduce.5.cloned.1.call-done = f32[256,1024]{1,0:T(8,128)} async-done(((f32[256,1024]{1,0:T(8,128)}), f32[256,1024]{1,0:T(8,128)}) %all-reduce.5.cloned.1.call-update) | async-done | bytes 1048592 | tf_op jit(solution)/shard_map/psum | solution.py:139
  328.9 2.3 copy.53
  (72 shorter events, 24.0 us)
Async XLA Ops:
  7.2 53.4 %all-gather.4.cloned.1.call-start = ((), (), s32[]{:S(2)}) async-start(), calls=%async_computation.7 | async-start | bytes 1310720 | tf_op jit(solution)/shard_map/all_gather | solution.py:84
  7.9 24.4 %collective-permute-start = (bf16[128,1024]{1,0:T(8,128)(2,1)}, bf16[128,1024]{1,0:T(8,128)(2,1)}, u32[]{:S(2)}, u32[]{:S(2)}) collective-permute-start(bf16[128,1024]{1,0:T(8,128)(2,1)} %param.11), channel_id=1, source_target_pairs={{0,2},{1,3},{4,6},{5,7},{8,10},{9,11},{12,14},{13,15},{16,18},{17,... | collective-permute-start | bytes 786440 | tf_op jit(solution)/shard_map/ppermute | solution.py:10
  13.5 18.9 %collective-permute-start.1 = (bf16[128,1024]{1,0:T(8,128)(2,1)}, bf16[128,1024]{1,0:T(8,128)(2,1)}, u32[]{:S(2)}, u32[]{:S(2)}) collective-permute-start(bf16[128,1024]{1,0:T(8,128)(2,1)} %param.11), channel_id=1, source_target_pairs={{0,1},{1,2},{2,3},{4,5},{5,6},{6,7},{8,9},{9,10},{10,11},{12,13},{... | collective-permute-start | bytes 786440 | tf_op jit(solution)/shard_map/ppermute | solution.py:10
  22.2 9.4 %copy-start.7 = (bf16[256,1024]{1,0:T(8,128)(2,1)S(1)}, bf16[256,1024]{1,0:T(8,128)(2,1)}, u32[]{:S(2)}) copy-start(bf16[256,1024]{1,0:T(8,128)(2,1)} %param.16) | copy-start | bytes 1572868
  25.9 6.5 %copy-start.9 = (bf16[128,1024]{1,0:T(8,128)(2,1)S(1)}, bf16[128,1024]{1,0:T(8,128)(2,1)}, u32[]{:S(2)}) copy-start(bf16[128,1024]{1,0:T(8,128)(2,1)} %param.11) | copy-start | bytes 786436
  25.9 30.4 %all-to-all-start = ((bf16[4,128,1024]{2,1,0:T(8,128)(2,1)}), bf16[4,128,1024]{2,1,0:T(8,128)(2,1)}, u32[]{:S(2)}, u32[]{:S(2)}) async-start(bf16[4,128,1024]{2,1,0:T(8,128)(2,1)} %bitcast.1), calls=%async_computation | async-start | bytes 2097152 | tf_op jit(solution)/shard_map/all_to_all | solution.py:94
  30.9 33.0 %all-gather.8.cloned.1.call-start = ((), (), s32[]{:S(2)}) async-start(), calls=%async_computation.9 | async-start | bytes 1310720 | tf_op jit(solution)/shard_map/all_gather | solution.py:82
  33.6 14.0 %copy-start.4 = (bf16[1,383,1024]{2,1,0:T(8,128)(2,1)}, bf16[1,383,1024]{2,1,0:T(8,128)(2,1)S(1)}, u32[]{:S(2)}) copy-start(bf16[1,383,1024]{2,1,0:T(8,128)(2,1)S(1)} %fusion.27) | copy-start | bytes 2353156
  56.3 28.7 %all-to-all-start.1 = ((bf16[4,128,1024]{2,1,0:T(8,128)(2,1)}), bf16[4,128,1024]{2,1,0:T(8,128)(2,1)S(1)}, u32[]{:S(2)}, u32[]{:S(2)}) async-start(bf16[4,128,1024]{2,1,0:T(8,128)(2,1)} %bitcast.6), calls=%async_computation.1 | async-start | bytes 2097152 | tf_op jit(solution)/shard_map/all_to_all | solution.py:93
  59.8 29.1 %all-gather.6.cloned.1.call-start = ((), (), s32[]{:S(2)}) async-start(), calls=%async_computation.8 | async-start | bytes 1310720 | tf_op jit(solution)/shard_map/all_gather | solution.py:83
  85.0 1.0 copy-start.1
  88.9 4.1 %copy-start = (bf16[1,1024,512]{2,1,0:T(8,128)(2,1)S(1)}, bf16[1,1024,512]{2,1,0:T(8,128)(2,1)}, u32[]{:S(2)}) copy-start(bf16[1,1024,512]{2,1,0:T(8,128)(2,1)} %all-gather.8.cloned.1.call-done) | copy-start | bytes 3145732
  93.0 0.8 copy-start.5
  93.0 3.3 copy-start.6
  93.0 1.6 copy-start.3
  96.3 28.7 %all-to-all-start.2 = ((bf16[4,128,1024]{2,1,0:T(8,128)(2,1)}), bf16[4,128,1024]{2,1,0:T(8,128)(2,1)S(1)}, u32[]{:S(2)}, u32[]{:S(2)}) async-start(bf16[4,128,1024]{2,1,0:T(8,128)(2,1)} %bitcast.65), calls=%async_computation.2 | async-start | bytes 2097152 | tf_op jit(solution)/shard_map/all_to_all | solution.py:102
  99.8 100.8 %all-reduce.3.cloned.1.call-start = ((), (), s32[]{:S(2)}) async-start(), calls=%async_computation.10 | async-start | bytes 2097152 | tf_op jit(solution)/shard_map/psum | solution.py:139
  153.5 3.3 copy-start.2
  153.6 65.0 %reduce-scatter.8.cloned.1.call-start = ((), (), s32[]{:S(2)}) async-start(), calls=%async_computation.14 | async-start | bytes 1310720 | tf_op jit(solution)/shard_map/reduce_scatter | solution.py:128
  156.8 89.7 %reduce-scatter.6.cloned.1.call-start = ((), (), s32[]{:S(2)}) async-start(), calls=%async_computation.13 | async-start | bytes 1310720 | tf_op jit(solution)/shard_map/reduce_scatter | solution.py:125
  159.7 115.0 %reduce-scatter.4.cloned.1.call-start = ((), (), s32[]{:S(2)}) async-start(), calls=%async_computation.12 | async-start | bytes 1310720 | tf_op jit(solution)/shard_map/reduce_scatter | solution.py:122
  165.6 28.7 %all-to-all-start.3 = ((bf16[4,128,1024]{2,1,0:T(8,128)(2,1)}), bf16[4,128,1024]{2,1,0:T(8,128)(2,1)S(1)}, u32[]{:S(2)}, u32[]{:S(2)}) async-start(bf16[4,128,1024]{2,1,0:T(8,128)(2,1)} %bitcast.71), calls=%async_computation.3 | async-start | bytes 2097152 | tf_op jit(solution)/shard_map/all_to_all | solution.py:109
  169.1 159.7 %all-reduce.5.cloned.1.call-start = ((), (), s32[]{:S(2)}) async-start(), calls=%async_computation.11 | async-start | bytes 2097152 | tf_op jit(solution)/shard_map/psum | solution.py:139
  169.2 30.3 %collective-permute-start.3 = (bf16[128,1024]{1,0:T(8,128)(2,1)S(1)}, bf16[128,1024]{1,0:T(8,128)(2,1)}, u32[]{:S(2)}, u32[]{:S(2)}) collective-permute-start(bf16[128,1024]{1,0:T(8,128)(2,1)S(1)} %reduce_sum.21), channel_id=1, source_target_pairs={{2,0},{3,1},{6,4},{7,5},{10,8},{11,9},{14,12},{15,13},{18,16},{19,... | collective-permute-start | bytes 786440 | tf_op jit(solution)/shard_map/ppermute | solution.py:10
  170.5 29.0 %collective-permute-start.2 = (bf16[128,1024]{1,0:T(8,128)(2,1)S(1)}, bf16[128,1024]{1,0:T(8,128)(2,1)}, u32[]{:S(2)}, u32[]{:S(2)}) collective-permute-start(bf16[128,1024]{1,0:T(8,128)(2,1)S(1)} %reduce_sum.21), channel_id=1, source_target_pairs={{1,0},{2,1},{3,2},{5,4},{6,5},{7,6},{9,8},{10,9},{11,10},{13,12},{... | collective-permute-start | bytes 786440 | tf_op jit(solution)/shard_map/ppermute | solution.py:10
  198.7 1.9 copy-start.8
Sparse Core Ops, SparseCore 0:
  9.6 19.4 all-gather.3
  33.3 17.2 all-gather.7
  62.2 17.1 all-gather.5
  153.7 36.1 all-reduce.2
  193.0 25.5 reduce-scatter.7
  221.5 24.9 reduce-scatter.5
  249.7 24.8 reduce-scatter.3
  277.0 51.8 all-reduce.4
